TPU v7x, 32 devices: a whole 2x2x4 slice. The times are simulated.
32 devices in a mesh: pix: 8 (over z, y), rep: 4 (over x, core).
Axes of the slice: x: 2, y: 2, z: 4, core: 2. Of those that a mesh axis runs over, the one named last changes fastest.
Arguments:
- sky_cube: float32 [4, 512, 65536], P('rep', None, 'pix'), may hold values from -6 to 10
- pixel_mask: int32 [4, 65536], P('rep', 'pix'), may hold values 0 or 1
- noise_cov: float32 [512, 512], replicated, may hold values from -1 to 2, as said below
Outputs:
- power_cube: float32 [4, 512, 65536], P('rep', 'pix')
Inputs may be any that keep to these rules, and one draw needn't show every extreme that they name: `noise_cov`: symmetric; each diagonal entry exceeds the sum of magnitudes off the diagonal in its row.
All inputs are finite; a program needn't handle non-finite values. No bound on the sum of `pixel_mask` on one device may be relied on, other than what follows from the above.
Results may differ from a plain program's by a relative error of at most 0.00012.
Values sent between devices are 32-bit elements; how exact they have to be, the bound alone decides.
A program may use at most 320 MiB of HBM per device.

v0:
```python
import math

import jax
import jax.numpy as jnp
from jax import lax
from jax.sharding import PartitionSpec as P

F = 512
SY = 256
SX = 256


HI = lax.Precision.HIGHEST


def dft_pair(length):
    idx = jnp.arange(length, dtype=jnp.int32)
    phase = (idx[:, None] * idx[None, :] % length).astype(jnp.float32) * (2.0 * math.pi / length)
    return (jnp.cos(phase), jnp.sin(phase))


def los_table(length):
    idx = jnp.arange(length, dtype=jnp.int32)
    half_len = length // 2
    freq = jnp.where(idx <= half_len, idx, idx - half_len)
    phase = (freq[:, None] * idx[None, :] % length).astype(jnp.float32) * (2.0 * math.pi / length)
    values = jnp.where((idx <= half_len)[:, None], jnp.cos(phase), jnp.sin(phase))
    edge = jnp.logical_or(idx == 0, idx == half_len)
    scale = jnp.where(edge, math.sqrt(1.0 / length), math.sqrt(2.0 / length)).astype(jnp.float32)
    return values * scale[:, None]


def sky_power(planes, rows_y, cols_x):
    count = planes.shape[0]
    field = planes.reshape(count, rows_y, cols_x)
    cos_x, sin_x = dft_pair(cols_x)
    cos_y, sin_y = dft_pair(rows_y)
    both_x = jnp.concatenate([cos_x, sin_x], axis=1)
    both_y = jnp.concatenate([cos_y, sin_y], axis=0)
    first = jnp.einsum("kyx,xw->kyw", field, both_x, precision=HI)
    second = jnp.einsum("vy,kyw->kvw", both_y, first, precision=HI)
    real_part = second[:, :rows_y, :cols_x] - second[:, rows_y:, cols_x:]
    imag_part = -(second[:, rows_y:, :cols_x] + second[:, :rows_y, cols_x:])
    power_map = (real_part * real_part + imag_part * imag_part) / float(rows_y * cols_x)
    return power_map.reshape(count, rows_y * cols_x)


def reduce_cov(partial_value):
    summed = lax.psum(partial_value, ("pix", "rep"))
    return summed


def plane_power(planes):
    return sky_power(planes[0], SY, SX)[None]


def local(sky_cube, pixel_mask, noise_cov):
    live = pixel_mask[0].astype(jnp.float32)
    masked = sky_cube[0] * live[None, :]
    table = los_table(F)
    partial_value = jnp.dot(masked, masked.T, precision=HI)
    data_cov = reduce_cov(partial_value)
    scale_all = float(lax.axis_size("pix") * lax.axis_size("rep") * masked.shape[1])
    regular = data_cov / scale_all + noise_cov
    factor = jnp.linalg.cholesky(regular)
    filter_t = jax.scipy.linalg.cho_solve((factor, True), noise_cov)
    folded_map = jnp.dot(table, filter_t.T, precision=HI)
    spectra = jnp.dot(folded_map, masked, precision=HI)
    owners = lax.axis_size("pix")
    stacked = spectra.reshape(owners, spectra.shape[0] // owners, spectra.shape[1])
    return plane_power(lax.all_to_all(stacked, "pix", split_axis=0, concat_axis=2, tiled=True))


def solution(mesh):
    placed = (P("rep", None, "pix"), P("rep", "pix"), P())
    return jax.shard_map(
        local, mesh=mesh, in_specs=placed, out_specs=P("rep", "pix", None), check_vma=False
    )
```

profile of v0, /device:TPU:0, one launch (start us, length us, event | category | flops | bytes accessed | tf_op | source)
XLA Modules:
  0.0 922.0 jit_solution(2023043148262930889)
XLA Ops:
  7.3 32.5 %fusion.6 = f32[512,512]{0,1:T(8,128)} fusion(f32[1,512,8192]{2,1,0:T(8,128)} %param.3, f32[8192]{0:T(1024)S(1)} %bitcast.88), kind=kOutput, calls=%fused_computation.11 | convolution fusion | flops 25773998080 | bytes 17858560 | tf_op jit(solution)/shard_map/dot_general | solution.py:61
  40.2 133.2 %all-reduce.3.cloned.1.call-done = f32[512,512]{0,1:T(8,128)} async-done(((f32[512,512]{0,1:T(8,128)}), f32[512,512]{0,1:T(8,128)}) %all-reduce.3.cloned.1.call-update) | async-done | bytes 1048592 | tf_op jit(solution)/shard_map/psum | solution.py:49
  173.5 1.4 multiply_add_fusion
  176.5 11.7 %cholesky.104 = f32[128,128]{1,0:T(8,128)S(1)} custom-call(f32[128,128]{1,0:T(8,128)S(1)} %cholesky.266), custom_call_target="Cholesky" | custom-call | tf_op jit(solution)/shard_map/jit(cholesky)/cholesky | solution.py:65
  188.2 9.8 %custom-call.34 = f32[1,128,128]{1,2,0:T(8,128)S(1)} custom-call(f32[1,128,128]{2,1,0:T(8,128)S(1)} %get-tuple-element.32), custom_call_target="InvertDiagBlocksLowerTriangular" | custom-call | tf_op jit(solution)/shard_map/jit(cholesky)/cholesky | solution.py:65
  198.2 1.2 constant_dynamic-update-slice_fusion.2
  199.4 1.3 convolution_subtract_fusion.6
  200.7 11.7 %cholesky.217 = f32[128,128]{1,0:T(8,128)S(1)} custom-call(f32[128,128]{1,0:T(8,128)S(1)} %cholesky.270), custom_call_target="Cholesky" | custom-call | tf_op jit(solution)/shard_map/jit(cholesky)/cholesky | solution.py:65
  212.4 10.2 %custom-call.35 = f32[1,128,128]{1,2,0:T(8,128)S(1)} custom-call(f32[1,128,128]{2,1,0:T(8,128)S(1)} %get-tuple-element.29), custom_call_target="InvertDiagBlocksLowerTriangular" | custom-call | tf_op jit(solution)/shard_map/jit(cholesky)/cholesky | solution.py:65
  222.9 1.3 convolution_subtract_fusion.7
  224.2 11.7 %cholesky.238 = f32[128,128]{1,0:T(8,128)S(1)} custom-call(f32[128,128]{1,0:T(8,128)S(1)} %cholesky.275), custom_call_target="Cholesky" | custom-call | tf_op jit(solution)/shard_map/jit(cholesky)/cholesky | solution.py:65
  236.7 9.8 %custom-call.36 = f32[1,128,128]{1,2,0:T(8,128)S(1)} custom-call(f32[1,128,128]{2,1,0:T(8,128)S(1)} %get-tuple-element.26), custom_call_target="InvertDiagBlocksLowerTriangular" | custom-call | tf_op jit(solution)/shard_map/jit(cholesky)/cholesky | solution.py:65
  246.7 1.2 convolution_subtract_fusion.8
  247.9 11.9 %cholesky.255 = f32[128,128]{1,0:T(8,128)S(1)} custom-call(f32[128,128]{1,0:T(8,128)S(1)} %convolution_subtract_fusion.8), custom_call_target="Cholesky" | custom-call | tf_op jit(solution)/shard_map/jit(cholesky)/cholesky | solution.py:65
  263.8 8.5 while.1
  264.5 1.4 bitcast_dynamic-update-slice_fusion.2
  266.6 1.4 bitcast_dynamic-update-slice_fusion.2
  268.7 1.4 bitcast_dynamic-update-slice_fusion.2
  270.8 1.4 bitcast_dynamic-update-slice_fusion.2
  272.3 39.3 %custom-call.37 = f32[4,128,128]{1,2,0:T(8,128)S(1)} custom-call(f32[4,128,128]{2,1,0:T(8,128)S(1)} %get-tuple-element.12), custom_call_target="InvertDiagBlocksLowerTriangular" | custom-call | tf_op jit(solution)/shard_map/jit(_cho_solve)/triangular_solve | solution.py:66
  317.8 6.1 fusion.15
  323.9 31.8 %fusion.4 = f32[8,64,8192]{2,1,0:T(8,128)} fusion(f32[8,64,512]{2,1,0:T(8,128)S(1)} %bitcast.87, f32[1,512,8192]{2,1,0:T(8,128)} %param.3, f32[8192]{0:T(1024)S(1)} %bitcast.89), kind=kOutput, calls=%fused_computation.9 | convolution fusion | flops 25773998080 | bytes 34635776 | tf_op jit(solution)/shard_map/dot_general | solution.py:68
  355.8 5.8 all-to-all-start
  361.6 1.0 fusion.80
  362.6 361.2 %all-to-all-done = f32[8,64,8192]{2,1,0:T(8,128)} async-done(((f32[8,64,8192]{2,1,0:T(8,128)}), f32[8,64,8192]{2,1,0:T(8,128)}, u32[]{:S(2)}, u32[]{:S(2)}) %all-to-all-start) | async-done | bytes 16777248 | tf_op jit(solution)/shard_map/all_to_all | solution.py:71
  723.8 17.8 %copy.10 = f32[1,64,8,8192]{3,2,1,0:T(8,128)} copy(f32[1,64,8,8192]{3,1,2,0:T(8,128)} %bitcast.16) | data formatting | bytes 33554432 | tf_op jit(solution)/shard_map/all_to_all | solution.py:71
  741.6 18.0 %reshape_squeeze.3 = f32[64,256,256]{2,1,0:T(8,128)} reshape(f32[1,64,8,8192]{3,2,1,0:T(8,128)} %copy.10) | data formatting | bytes 33554432 | tf_op jit(solution)/shard_map/reshape;squeeze | solution.py:35
  759.6 33.6 %fusion.50 = f32[64,256,512]{1,2,0:T(8,128)} fusion(f32[64,256,256]{2,1,0:T(8,128)} %reshape_squeeze.3, f32[256,256]{1,0:T(8,128)S(1)} %get-tuple-element.37, f32[256,256]{1,0:T(8,128)S(1)} %get-tuple-element.38), kind=kOutput, calls=%fused_computation.71 | convolution fusion | flops 25769934848 | bytes 50855936 | tf_op jit(solution)/shard_map/kyx,xw->kyw/dot_general | solution.py:40
  793.2 61.1 %convolution_bitcast_fusion = f32[64,512,512]{1,2,0:T(8,128)} fusion(f32[64,256,512]{1,2,0:T(8,128)} %fusion.50, f32[512,256,1]{1,0,2:T(8,128)S(1)} %maximum_bitcast_fusion.6), kind=kOutput, calls=%fused_computation.2 | convolution fusion | flops 51539607552 | bytes 101187584 | tf_op jit(solution)/shard_map/vy,kyw->kvw/dot_general | solution.py:41
  854.3 28.6 %fusion.2 = f32[64,256,256]{1,2,0:T(8,128)} fusion(f32[64,512,512]{1,2,0:T(8,128)} %convolution_bitcast_fusion), kind=kLoop, calls=%fused_computation.6 | loop fusion | flops 25165824 | bytes 83886080 | tf_op jit(solution)/shard_map/div | solution.py:44
  882.9 17.5 %copy.11 = f32[64,256,256]{2,1,0:T(8,128)} copy(f32[64,256,256]{1,2,0:T(8,128)} %fusion.2) | data formatting | bytes 33554432 | tf_op jit(solution)/shard_map/div | solution.py:44
  900.4 14.6 %broadcast_in_dim_reshape.3 = f32[1,64,65536]{2,1,0:T(8,128)} reshape(f32[64,256,256]{2,1,0:T(8,128)} %copy.11) | data formatting | bytes 33554432 | tf_op jit(solution)/shard_map/broadcast_in_dim;reshape | solution.py:54
  (53 shorter events, 14.4 us)
Async XLA Ops:
  6.5 166.9 %all-reduce.3.cloned.1.call-start = ((), (), s32[]{:S(2)}) async-start(), calls=%async_computation.1 | async-start | bytes 2097152 | tf_op jit(solution)/shard_map/psum | solution.py:49
  7.3 32.5 %copy-start = (f32[512,512]{1,0:T(8,128)S(1)}, f32[512,512]{1,0:T(8,128)}, u32[]{:S(2)}) copy-start(f32[512,512]{1,0:T(8,128)} %param.5) | copy-start | bytes 3145732
  175.5 1.0 copy-start.1
  355.8 368.0 %all-to-all-start = ((f32[8,64,8192]{2,1,0:T(8,128)}), f32[8,64,8192]{2,1,0:T(8,128)}, u32[]{:S(2)}, u32[]{:S(2)}) async-start(f32[8,64,8192]{2,1,0:T(8,128)} %fusion.4), calls=%async_computation | async-start | bytes 33554432 | tf_op jit(solution)/shard_map/all_to_all | solution.py:71
Sparse Core Ops, SparseCore 0:
  40.0 133.4 all-reduce.2
where the time goes:
time: 929 us; the launch traced here: 922 us
  waiting for transfers between devices  494 us (53%)
  matrix products  177 us (19%)
  other arithmetic  151 us (16%)
  local copies, waits for them, and re-layouts  78 us (8%)
  between operations  16.5 us (2%)
    all_to_all x1, waiting for transfers between devices, local(): lax.all_to_all(stacked, 'pix', split_axis=0, concat_axis=2, tiled=True)  361 us
    psum x1, waiting for transfers between devices, reduce_cov(): summed = lax.psum(partial_value, ('pix', 'rep'))  133 us
    another operation x14, other arithmetic, local(): factor = jnp.linalg.cholesky(regular)  79 us
    dot_general x1, matrix products, sky_power(): second = jnp.einsum('vy,kyw->kvw', both_y, first, precision=HI)  61.1 us
    another operation x3, other arithmetic, local(): filter_t = jax.scipy.linalg.cho_solve((factor, True), noise_cov)  39.4 us
    dot_general x1, matrix products, sky_power(): first = jnp.einsum('kyx,xw->kyw', field, both_x, precision=HI)  33.6 us
    dot_general x1, matrix products, local(): partial_value = jnp.dot(masked, masked.T, precision=HI)  32.5 us
    dot_general x1, matrix products, local(): spectra = jnp.dot(folded_map, masked, precision=HI)  31.8 us
  transfers between devices with their start and end apart: 2, of which 2 were waited for; matrix products, arithmetic and copies ran while one was open for 0% of the time, Pallas kernels for 0%

commit v1 on v0

v1 whole, which is shorter than its diff:
```python
import functools
import math

import jax
import jax.numpy as jnp
import numpy as np
from jax import lax
from jax.experimental import pallas as pl
from jax.experimental.pallas import tpu as pltpu
from jax.sharding import PartitionSpec as P

F = 512
SY = 256
SX = 256
BLOCK = 128

HI = lax.Precision.HIGHEST
MID = lax.Precision.HIGH
MESH = pl.DeviceIdType.MESH


def dft_pair(length):
    idx = jnp.arange(length, dtype=jnp.int32)
    phase = (idx[:, None] * idx[None, :] % length).astype(jnp.float32) * (2.0 * math.pi / length)
    return (jnp.cos(phase), jnp.sin(phase))


def los_table(length):
    idx = np.arange(length)
    half_len = length // 2
    freq = np.where(idx <= half_len, idx, idx - half_len)
    phase = (freq[:, None] * idx[None, :] % length) * (2.0 * math.pi / length)
    values = np.where((idx <= half_len)[:, None], np.cos(phase), np.sin(phase))
    edge = np.logical_or(idx == 0, idx == half_len)
    scale = np.where(edge, math.sqrt(1.0 / length), math.sqrt(2.0 / length))
    return (values * scale[:, None]).astype(np.float32)


def sky_power(planes, rows_y, cols_x):
    count = planes.shape[0]
    field = planes.reshape(count, rows_y, cols_x)
    cos_x, sin_x = dft_pair(cols_x)
    cos_y, sin_y = dft_pair(rows_y)
    both_x = jnp.concatenate([cos_x, sin_x], axis=1)
    both_y = jnp.concatenate([cos_y, sin_y], axis=0)
    first = jnp.einsum("kyx,xw->kyw", field, both_x, precision=MID)
    second = jnp.einsum("vy,kyw->kvw", both_y, first, precision=MID)
    real_part = second[:, :rows_y, :cols_x] - second[:, rows_y:, cols_x:]
    imag_part = -(second[:, rows_y:, :cols_x] + second[:, :rows_y, cols_x:])
    power_map = (real_part * real_part + imag_part * imag_part) / float(rows_y * cols_x)
    return power_map.reshape(count, rows_y * cols_x)


def sum_kernel(axes, x_ref, o_ref, acc, full, got, send_sem, recv_sem):
    where = {name: lax.axis_index(name) for name, _ in axes}
    steps = []
    for name, size in axes:
        bit = 1
        while bit < size:
            steps.append((name, bit))
            bit *= 2

    def partner(name, bit):
        me = where[name]
        mine = lax.rem(me // bit, 2)
        return mine, {name: me + bit * (1 - 2 * mine)}

    barrier = pltpu.get_barrier_semaphore()
    for name, bit in steps:
        _, other = partner(name, bit)
        pl.semaphore_signal(barrier, inc=1, device_id=other, device_id_type=MESH)
    pl.semaphore_wait(barrier, len(steps))

    total = x_ref.shape[0]
    rows, start, offset = total, 0, 0
    acc[...] = x_ref[...]
    plan = []
    for n, (name, bit) in enumerate(steps):
        mine, other = partner(name, bit)
        split = rows % 16 == 0
        if split:
            rows //= 2
            away = start + (1 - mine) * rows
            start = start + mine * rows
        else:
            away = start
        plan.append((other, split, start, rows, mine))
        if split:
            away = pl.multiple_of(away, 8)
        here = pl.multiple_of(start, 8)
        source = x_ref if n == 0 else acc
        copy = pltpu.make_async_remote_copy(
            src_ref=source.at[pl.ds(away, rows)],
            dst_ref=got.at[pl.ds(offset, rows)],
            send_sem=send_sem.at[n],
            recv_sem=recv_sem.at[n],
            device_id=other,
            device_id_type=MESH,
        )
        copy.start()
        copy.wait()
        acc[pl.ds(here, rows)] = acc[pl.ds(here, rows)] + got[pl.ds(offset, rows)]
        offset += rows
    last = pl.ds(pl.multiple_of(start, 8), rows)
    full[last] = acc[last]
    for n in reversed(range(len(steps))):
        other, split, start, rows, mine = plan[n]
        if not split:
            continue
        here = pl.multiple_of(start, 8)
        copy = pltpu.make_async_remote_copy(
            src_ref=full.at[pl.ds(here, rows)],
            dst_ref=full.at[pl.ds(here, rows)],
            send_sem=send_sem.at[len(steps) + n],
            recv_sem=recv_sem.at[len(steps) + n],
            device_id=other,
            device_id_type=MESH,
        )
        copy.start()
        copy.wait()
    o_ref[...] = full[...]


def reduce_cov(partial_value, sizes):
    axes = [("rep", sizes["rep"]), ("pix", sizes["pix"])]
    rows, depth, count = partial_value.shape[0], 0, 0
    for _, size in axes:
        for _ in range(size.bit_length() - 1):
            if rows % 16 == 0:
                rows //= 2
            depth += rows
            count += 1
    vmem = pl.BlockSpec(memory_space=pltpu.VMEM)
    return pl.pallas_call(
        functools.partial(sum_kernel, axes),
        out_shape=jax.ShapeDtypeStruct(partial_value.shape, jnp.float32),
        in_specs=[vmem],
        out_specs=vmem,
        scratch_shapes=[
            pltpu.VMEM(partial_value.shape, jnp.float32),
            pltpu.VMEM(partial_value.shape, jnp.float32),
            pltpu.VMEM((depth, partial_value.shape[1]), jnp.float32),
            pltpu.SemaphoreType.DMA((2 * count,)),
            pltpu.SemaphoreType.DMA((2 * count,)),
        ],
        compiler_params=pltpu.CompilerParams(collective_id=0, has_side_effects=True),
        name="cov_sum",
    )(partial_value)


def block_inverse(a):
    size = a.shape[0]
    row_id = lax.broadcasted_iota(jnp.int32, (size, size), 0)
    col_id = lax.broadcasted_iota(jnp.int32, (size, size), 1)
    for j in range(size):
        pivot = 1.0 / a[j : j + 1, j : j + 1]
        row = a[j : j + 1, :] * pivot
        col = a[:, j : j + 1]
        base = jnp.where(col_id == j, 0.0, a)
        row = jnp.where(col_id[:1] == j, pivot, row)
        a = jnp.where(row_id == j, row, base - col * row)
    return a


def solve_kernel(scale, cov_ref, noise_ref, table_ref, o_ref, a_ref):
    size = cov_ref.shape[0]
    a_ref[...] = cov_ref[...] * scale + noise_ref[...]
    o_ref[...] = lax.dot_general(
        noise_ref[...],
        table_ref[...],
        (((1,), (1,)), ((), ())),
        precision=HI,
        preferred_element_type=jnp.float32,
    )
    blocks = size // BLOCK

    def mul(x, y):
        return jnp.dot(x, y, precision=HI, preferred_element_type=jnp.float32)

    def step(k, _):
        here = pl.ds(pl.multiple_of(k * BLOCK, BLOCK), BLOCK)
        inverse = block_inverse(a_ref[here, here])
        panel = mul(inverse, a_ref[here, :])
        right = mul(inverse, o_ref[here, :])
        for i in range(blocks):
            rows = pl.ds(i * BLOCK, BLOCK)

            @pl.when(k != i)
            def _():
                factor = a_ref[rows, here]
                o_ref[rows, :] = o_ref[rows, :] - mul(factor, right)

                @pl.when(k < blocks - 1)
                def _():
                    a_ref[rows, :] = a_ref[rows, :] - mul(factor, panel)

        o_ref[here, :] = right
        a_ref[here, :] = panel
        return 0

    lax.fori_loop(0, blocks, step, 0)


def folded_transpose(data_cov, scale, noise_cov, table):
    vmem = pl.BlockSpec(memory_space=pltpu.VMEM)
    return pl.pallas_call(
        functools.partial(solve_kernel, scale),
        out_shape=jax.ShapeDtypeStruct(data_cov.shape, jnp.float32),
        in_specs=[vmem] * 3,
        out_specs=vmem,
        scratch_shapes=[pltpu.VMEM(data_cov.shape, jnp.float32)],
        name="filter_solve",
    )(data_cov, noise_cov, table)


def local(sizes, sky_cube, pixel_mask, noise_cov):
    live = pixel_mask[0].astype(jnp.float32)
    masked = sky_cube[0] * live[None, :]
    table = jnp.asarray(los_table(F))
    partial_value = jnp.dot(masked, masked.T, precision=MID)
    data_cov = reduce_cov(partial_value, sizes)
    count_all = sizes["pix"] * sizes["rep"] * masked.shape[1]
    folded = folded_transpose(data_cov, 1.0 / count_all, noise_cov, table).T
    owners = sizes["pix"]
    share = F // owners
    eighth = share // 8
    widths = [eighth, 2 * eighth, 2 * eighth, 2 * eighth, eighth] if eighth else [share]
    by_owner = folded.reshape(owners, share, F)
    result, planes = None, []

    def place(done, at, result):
        power = sky_power(planes[done][0], SY, SX)
        if result is None:
            return jnp.pad(power, ((at, share - at - power.shape[0]), (0, 0)))
        return lax.dynamic_update_slice(result, power, (at, 0))

    starts = [sum(widths[:c]) for c in range(len(widths))]
    for c, width in enumerate(widths):
        rows = by_owner[:, starts[c] : starts[c] + width].reshape(owners * width, F)
        spectra = jnp.dot(rows, masked, precision=MID)
        stacked = spectra.reshape(owners, width, spectra.shape[1])
        if c >= 2:
            result = place(c - 2, starts[c - 2], result)
            stacked, result = lax.optimization_barrier((stacked, result))
        planes.append(lax.all_to_all(stacked, "pix", split_axis=0, concat_axis=2, tiled=True))
    for done in range(max(0, len(widths) - 2), len(widths)):
        result = place(done, starts[done], result)
    return result[None]


def solution(mesh):
    placed = (P("rep", None, "pix"), P("rep", "pix"), P())
    return jax.shard_map(
        functools.partial(local, dict(mesh.shape)),
        mesh=mesh,
        in_specs=placed,
        out_specs=P("rep", "pix", None),
        check_vma=False,
    )
```

time: 929 us -> 568 us (0.61)
  waiting for transfers between devices: 494 us -> 193 us
  other arithmetic: 151 us -> 14.1 us
  Pallas kernels: 0 us -> 104 us
  matrix products: 177 us -> 126 us
  local copies, waits for them, and re-layouts: 78 us -> 98.3 us
  starting transfers between devices: 5.76 us -> 24.3 us
  between operations: 16.5 us -> 0.42 us
    all_to_all x1 -> x5, waiting for transfers between devices: 361 us -> 193 us  [local(): lax.all_to_all(stacked, 'pix', split_axis=0, concat_axis=2, tiled=True)]
    psum x1 -> x0, waiting for transfers between devices: 133 us -> none  [reduce_cov(): summed = lax.psum(partial_value, ('pix', 'rep'))]
    another operation x17 -> x0, other arithmetic: 118 us -> none  [the longest x14 79 us: local(): factor = jnp.linalg.cholesky(regular)]
    pallas_call x0 -> x2, Pallas kernels: none -> 104 us  [the longest x1 59.4 us: folded_transpose(): pl.pallas_call(functools.partial(solve_kernel, scale), out_shape=jax.Shap...]
    dot_general x5 -> x16, matrix products: 165 us -> 126 us  [the longest x5 56.4 us: local(): spectra = jnp.dot(rows, masked, precision=MID)]
    another operation x18 -> x0, local copies, waits for them, and re-layouts: 23.1 us -> none  [the longest x1 14.6 us: plane_power(): return sky_power(planes[0], SY, SX)[None]]
    all_to_all x1 -> x5, starting transfers between devices: 5.76 us -> 24.3 us  [local(): lax.all_to_all(stacked, 'pix', split_axis=0, concat_axis=2, tiled=True)]
    div x1 -> x5, other arithmetic: 28.6 us -> 12.3 us  [sky_power(): (real_part * real_part + imag_part * imag_part) / float(rows_y * cols_x)]
  transfers between devices with their start and end apart: 2 -> 5, of which waited for: 2 -> 5; matrix products, arithmetic and copies ran while one was open for 0% -> 32% of each run, Pallas kernels for 0% -> 0%
where the time goes in v1:
time: 568 us; the launch traced here: 560 us
  waiting for transfers between devices  193 us (34%)
  matrix products  126 us (22%)
  Pallas kernels  104 us (18%)
  local copies, waits for them, and re-layouts  98.3 us (17%)
  starting transfers between devices  24.3 us (4%)
  other arithmetic  14.1 us (2%)
    all_to_all x5, waiting for transfers between devices, local(): lax.all_to_all(stacked, 'pix', split_axis=0, concat_axis=2, tiled=True)  193 us
    pallas_call x1, Pallas kernels, folded_transpose(): pl.pallas_call(functools.partial(solve_kernel, scale), out_shape=jax.Shap...  59.4 us
    dot_general x5, matrix products, local(): spectra = jnp.dot(rows, masked, precision=MID)  56.4 us
    pallas_call x1, Pallas kernels, reduce_cov(): pl.pallas_call(functools.partial(sum_kernel, axes), out_shape=jax.ShapeDt...  45 us
    dot_general x5, matrix products, sky_power(): second = jnp.einsum('vy,kyw->kvw', both_y, first, precision=MID)  27.6 us
    all_to_all x5, local copies, waits for them, and re-layouts, local(): lax.all_to_all(stacked, 'pix', split_axis=0, concat_axis=2, tiled=True)  26.6 us
    all_to_all x5, starting transfers between devices, local(): lax.all_to_all(stacked, 'pix', split_axis=0, concat_axis=2, tiled=True)  24.3 us
    dot_general x5, matrix products, sky_power(): first = jnp.einsum('kyx,xw->kyw', field, both_x, precision=MID)  21.4 us
  transfers between devices with their start and end apart: 5, of which 5 were waited for; matrix products, arithmetic and copies ran while one was open for 32% of the time, Pallas kernels for 0%

profile of v1, /device:TPU:0, one launch (start us, length us, event | category | flops | bytes accessed | tf_op | source)
XLA Modules:
  0.0 560.0 jit_solution(18082126265627763637)
XLA Ops:
  0.8 20.3 %fusion.10.x_ref = f32[512,512]{1,0:T(8,128)} fusion(f32[1,512,8192]{2,1,0:T(8,128)} %param.4, f32[8192]{0:T(1024)S(1)} %bitcast.101), kind=kOutput, calls=%fused_computation.10 | convolution fusion | flops 12889096192 | bytes 17858560 | tf_op jit(solution)/shard_map/dot_general | solution.py:220
  21.1 45.0 %cov_sum.1.cov_ref = f32[512,512]{1,0:T(8,128)} custom-call(f32[512,512]{1,0:T(8,128)} %fusion.10.x_ref), custom_call_target="tpu_custom_call" | custom-call | tf_op jit(solution)/shard_map/cov_sum/pallas_call | solution.py:134
  66.1 59.4 %filter_solve.1 = f32[512,512]{1,0:T(8,128)} custom-call(f32[512,512]{1,0:T(8,128)} %cov_sum.1.cov_ref, f32[512,512]{1,0:T(8,128)} %noise_ref.1, f32[512,512]{1,0:T(8,128)} %constant.67.clone.table_ref), custom_call_target="tpu_custom_call" | custom-call | tf_op jit(solution)/shard_map/filter_solve/pallas_call | solution.py:206
  127.0 10.8 %fusion.2 = f32[8,8,8192]{2,1,0:T(8,128)} fusion(f32[1,512,8192]{2,1,0:T(8,128)} %param.4, f32[8192]{0:T(1024)S(1)} %bitcast.102, f32[8,64,512]{2,1,0:T(8,128)S(1)} %bitcast.95), kind=kOutput, calls=%fused_computation.2 | convolution fusion | flops 1614807040 | bytes 19038208 | tf_op jit(solution)/shard_map/dot_general | solution.py:240
  137.9 5.5 all-to-all-start
  143.4 12.7 %fusion = f32[8,16,8192]{2,1,0:T(8,128)} fusion(f32[1,512,8192]{2,1,0:T(8,128)} %param.4, f32[8192]{0:T(1024)S(1)} %bitcast.103, f32[8,64,512]{2,1,0:T(8,128)} %bitcast.96), kind=kOutput, calls=%fused_computation | convolution fusion | flops 3225419776 | bytes 21266432 | tf_op jit(solution)/shard_map/dot_general | solution.py:240
  156.0 36.1 %all-to-all-done = f32[8,8,8192]{2,1,0:T(8,128)S(1)} async-done(((f32[8,8,8192]{2,1,0:T(8,128)}), f32[8,8,8192]{2,1,0:T(8,128)S(1)}, u32[]{:S(2)}, u32[]{:S(2)}) %all-to-all-start) | async-done | bytes 2097184 | tf_op jit(solution)/shard_map/all_to_all | solution.py:245
  193.5 4.8 all-to-all-start.1
  199.3 12.5 %fusion.8 = f32[8,8,8192]{2,1,0:T(8,128)} fusion(f32[1,512,8192]{2,1,0:T(8,128)} %param.4, f32[8192]{0:T(1024)S(1)} %bitcast.104, f32[8,64,512]{2,1,0:T(8,128)} %bitcast.97), kind=kOutput, calls=%fused_computation.8 | convolution fusion | flops 1614807040 | bytes 19038208 | tf_op jit(solution)/shard_map/dot_general | solution.py:240
  211.8 12.8 %fusion.4 = f32[8,16,8192]{2,1,0:T(8,128)} fusion(f32[1,512,8192]{2,1,0:T(8,128)} %param.4, f32[8192]{0:T(1024)S(1)} %bitcast.105, f32[8,64,512]{2,1,0:T(8,128)} %bitcast.98), kind=kOutput, calls=%fused_computation.4 | convolution fusion | flops 3225419776 | bytes 21266432 | tf_op jit(solution)/shard_map/dot_general | solution.py:240
  224.6 7.6 %fusion.6 = f32[8,16,8192]{2,1,0:T(8,128)} fusion(f32[1,512,8192]{2,1,0:T(8,128)S(1)} %bitcast.86, f32[8192]{0:T(1024)S(1)} %bitcast.106, f32[8,64,512]{2,1,0:T(8,128)} %bitcast.99), kind=kOutput, calls=%fused_computation.6 | convolution fusion | flops 3225419776 | bytes 21266432 | tf_op jit(solution)/shard_map/dot_general | solution.py:240
  249.0 7.2 %pad.4 = f32[64,65536]{1,0:T(8,128)} pad(f32[8,65536]{1,0:T(8,128)S(1)} %bitcast.94, f32[]{:T(128)} %constant.62.clone.1), padding=0_56x0_0 | pad | bytes 18874372 | tf_op jit(solution)/shard_map/jit(_pad)/pad | solution.py:234
  256.2 34.8 %all-to-all-done.1 = f32[8,16,8192]{2,1,0:T(8,128)} async-done(((f32[8,16,8192]{2,1,0:T(8,128)}), f32[8,16,8192]{2,1,0:T(8,128)}, u32[]{:S(2)}, u32[]{:S(2)}) %all-to-all-start.1) | async-done | bytes 4194336 | tf_op jit(solution)/shard_map/all_to_all | solution.py:245
  291.1 5.1 all-to-all-start.2
  296.2 6.6 %copy.13 = f32[1,16,8,8192]{3,2,1,0:T(8,128)} copy(f32[1,16,8,8192]{3,1,2,0:T(8,128)} %bitcast.11) | data formatting | bytes 8388608 | tf_op jit(solution)/shard_map/all_to_all | solution.py:245
  302.7 4.9 reshape_squeeze.16
  307.6 5.3 fusion.56
  312.9 6.7 %convolution_bitcast_fusion.2 = f32[16,512,512]{1,2,0:T(8,128)S(1)} fusion(f32[16,256,512]{1,2,0:T(8,128)S(1)} %fusion.56, f32[256,256]{1,0:T(8,128)S(1)} %get-tuple-element.17, f32[256,256]{1,0:T(8,128)S(1)} %get-tuple-element.18), kind=kOutput, calls=%fused_computation.20 | convolution fusion | flops 6442582016 | bytes 25690112 | tf_op jit(solution)/shard_map/vy,kyw->kvw/dot_general | solution.py:47
  323.3 5.5 copy.22
  333.2 55.4 %all-to-all-done.2 = f32[8,16,8192]{2,1,0:T(8,128)} async-done(((f32[8,16,8192]{2,1,0:T(8,128)}), f32[8,16,8192]{2,1,0:T(8,128)}, u32[]{:S(2)}, u32[]{:S(2)}) %all-to-all-start.2) | async-done | bytes 4194336 | tf_op jit(solution)/shard_map/all_to_all | solution.py:245
  393.2 6.5 %copy.15 = f32[1,16,8,8192]{3,2,1,0:T(8,128)} copy(f32[1,16,8,8192]{3,1,2,0:T(8,128)} %bitcast.14) | data formatting | bytes 8388608 | tf_op jit(solution)/shard_map/all_to_all | solution.py:245
  399.7 4.9 reshape_squeeze.17
  404.7 5.3 fusion.55
  410.0 6.7 %convolution_bitcast_fusion.1 = f32[16,512,512]{1,2,0:T(8,128)S(1)} fusion(f32[16,256,512]{1,2,0:T(8,128)S(1)} %fusion.55, f32[256,256]{1,0:T(8,128)S(1)} %get-tuple-element.17, f32[256,256]{1,0:T(8,128)S(1)} %get-tuple-element.18), kind=kOutput, calls=%fused_computation.19 | convolution fusion | flops 6442582016 | bytes 25690112 | tf_op jit(solution)/shard_map/vy,kyw->kvw/dot_general | solution.py:47
  420.6 5.4 copy.23
  430.5 55.2 %all-to-all-done.3 = f32[8,16,8192]{2,1,0:T(8,128)} async-done(((f32[8,16,8192]{2,1,0:T(8,128)}), f32[8,16,8192]{2,1,0:T(8,128)}, u32[]{:S(2)}, u32[]{:S(2)}) %all-to-all-start.3) | async-done | bytes 4194336 | tf_op jit(solution)/shard_map/all_to_all | solution.py:245
  490.1 6.6 %copy.17 = f32[1,16,8,8192]{3,2,1,0:T(8,128)} copy(f32[1,16,8,8192]{3,1,2,0:T(8,128)} %bitcast.18) | data formatting | bytes 8388608 | tf_op jit(solution)/shard_map/all_to_all | solution.py:245
  496.7 4.9 reshape_squeeze.18
  501.6 5.3 fusion.54
  506.9 6.7 %convolution_bitcast_fusion = f32[16,512,512]{1,2,0:T(8,128)S(1)} fusion(f32[16,256,512]{1,2,0:T(8,128)S(1)} %fusion.54, f32[256,256]{1,0:T(8,128)S(1)} %get-tuple-element.17, f32[256,256]{1,0:T(8,128)S(1)} %get-tuple-element.18), kind=kOutput, calls=%fused_computation.18 | convolution fusion | flops 6442582016 | bytes 25690112 | tf_op jit(solution)/shard_map/vy,kyw->kvw/dot_general | solution.py:47
  517.3 5.4 copy.18
  526.6 11.3 %all-to-all-done.4 = f32[8,8,8192]{2,1,0:T(8,128)} async-done(((f32[8,8,8192]{2,1,0:T(8,128)}), f32[8,8,8192]{2,1,0:T(8,128)}, u32[]{:S(2)}, u32[]{:S(2)}) %all-to-all-start.4) | async-done | bytes 2097184 | tf_op jit(solution)/shard_map/all_to_all | solution.py:245
  (40 shorter events, 76.3 us)
Async XLA Ops:
  127.0 10.8 %copy-start.1 = (f32[512,512]{1,0:T(8,128)}, f32[512,512]{1,0:T(8,128)S(1)}, u32[]{:S(2)}) copy-start(f32[512,512]{1,0:T(8,128)S(1)} %copy.10) | copy-start | bytes 3145732
  137.9 54.3 %all-to-all-start = ((f32[8,8,8192]{2,1,0:T(8,128)}), f32[8,8,8192]{2,1,0:T(8,128)S(1)}, u32[]{:S(2)}, u32[]{:S(2)}) async-start(f32[8,8,8192]{2,1,0:T(8,128)} %fusion.2), calls=%async_computation | async-start | bytes 4194304 | tf_op jit(solution)/shard_map/all_to_all | solution.py:245
  192.1 1.3 copy-start
  193.5 97.6 %all-to-all-start.1 = ((f32[8,16,8192]{2,1,0:T(8,128)}), f32[8,16,8192]{2,1,0:T(8,128)}, u32[]{:S(2)}, u32[]{:S(2)}) async-start(f32[8,16,8192]{2,1,0:T(8,128)} %fusion), calls=%async_computation.1 | async-start | bytes 8388608 | tf_op jit(solution)/shard_map/all_to_all | solution.py:245
  199.3 25.3 %slice-start = ((s8[16777216]{0:T(1024)(128)(4,1)}), s8[4194304]{0:T(1024)(128)(4,1)S(1)}, s32[]{:S(2)}) async-start(s8[16777216]{0:T(1024)(128)(4,1)} %bitcast.85), calls=%async_computation.5 | async-start | bytes 8388608
  199.3 25.3 %slice-start.1 = ((s8[16777216]{0:T(1024)(128)(4,1)}), s8[4194304]{0:T(1024)(128)(4,1)S(1)}, s32[]{:S(2)}) async-start(s8[16777216]{0:T(1024)(128)(4,1)} %bitcast.85), calls=%async_computation.6 | async-start | bytes 8388608
  199.3 25.3 %slice-start.2 = ((s8[16777216]{0:T(1024)(128)(4,1)}), s8[4194304]{0:T(1024)(128)(4,1)S(1)}, s32[]{:S(2)}) async-start(s8[16777216]{0:T(1024)(128)(4,1)} %bitcast.85), calls=%async_computation.7 | async-start | bytes 8388608
  211.8 12.8 %slice-start.3 = ((s8[16777216]{0:T(1024)(128)(4,1)}), s8[4194304]{0:T(1024)(128)(4,1)S(1)}, s32[]{:S(2)}) async-start(s8[16777216]{0:T(1024)(128)(4,1)} %bitcast.85), calls=%async_computation.8 | async-start | bytes 8388608
  291.1 97.6 %all-to-all-start.2 = ((f32[8,16,8192]{2,1,0:T(8,128)}), f32[8,16,8192]{2,1,0:T(8,128)}, u32[]{:S(2)}, u32[]{:S(2)}) async-start(f32[8,16,8192]{2,1,0:T(8,128)} %fusion.4), calls=%async_computation.2 | async-start | bytes 8388608 | tf_op jit(solution)/shard_map/all_to_all | solution.py:245
  388.6 97.1 %all-to-all-start.3 = ((f32[8,16,8192]{2,1,0:T(8,128)}), f32[8,16,8192]{2,1,0:T(8,128)}, u32[]{:S(2)}, u32[]{:S(2)}) async-start(f32[8,16,8192]{2,1,0:T(8,128)} %fusion.6), calls=%async_computation.3 | async-start | bytes 8388608 | tf_op jit(solution)/shard_map/all_to_all | solution.py:245
  485.7 52.2 %all-to-all-start.4 = ((f32[8,8,8192]{2,1,0:T(8,128)}), f32[8,8,8192]{2,1,0:T(8,128)}, u32[]{:S(2)}, u32[]{:S(2)}) async-start(f32[8,8,8192]{2,1,0:T(8,128)} %fusion.8), calls=%async_computation.4 | async-start | bytes 4194304 | tf_op jit(solution)/shard_map/all_to_all | solution.py:245
